TPU v7x, 32 devices: a whole 2x2x4 slice. The times are simulated.
32 devices in a mesh: gx: 8 (over z, x), gy: 4 (over y, core).
Axes of the slice: x: 2, y: 2, z: 4, core: 2. Of those that a mesh axis runs over, the one named last changes fastest.
Arguments:
- velocity: float32 [3, 64, 256, 128], P(None, 'gx', 'gy'), may hold values from -2 to 3, as said below
- counts: int32 [8, 4, 9], P('gx', 'gy'), may hold values from 1 to 1024, as said below
- src_cell: int32 [8, 4, 9, 1024], P('gx', 'gy'), may hold values from 0 to 65535
- weights: float32 [8, 4, 9, 1024], P('gx', 'gy'), may hold values from 0.05 to 0.35
- dst_cell: int32 [8, 4, 9, 1024], P('gx', 'gy'), may hold values from 0 to 65535
- blade_tile: int32 [20, 192], replicated, may hold values from 0 to 31, as said below
- blade_cell: int32 [20, 192], replicated, may hold values from 0 to 65535
- blade_coef: float32 [20, 192], replicated, may hold values from 0.5 to 2
Outputs:
- updated: float32 [3, 64, 256, 128], P(None, 'gx', 'gy')
- forcing: float32 [3, 64, 256, 128], P(None, 'gx', 'gy')
Inputs may be any that keep to these rules, and one draw needn't show every extreme that they name: The velocity components, streamwise with a mean near 1. `counts`: some list is full, with 1024 used slots. `blade_tile`: turbines stand near one spanwise row of tiles; a turbine's points lie in at most three tiles.
All inputs are finite; a program needn't handle non-finite values.
Results may differ from a plain program's by a relative error of at most 0.00002.
Values sent between devices are 32-bit elements; how exact they have to be, the bound alone decides.
No kernel may reach another device: no remote copies, remote signals or barrier semaphores. Data moves between devices by JAX's collectives and lax.ppermute only.
A program may use at most 256 MiB of HBM per device.

v0:
```python
import jax
import jax.numpy as jnp
from jax import lax
from jax.sharding import PartitionSpec as P


def padded_2(cells, sides, width):
    for axis, dim in sides:
        count = lax.axis_size(axis)
        head = lax.slice_in_dim(cells, 0, width, axis=dim)
        tail = lax.slice_in_dim(cells, cells.shape[dim] - width, cells.shape[dim], axis=dim)
        cells = jnp.concatenate(
            [
                lax.ppermute(tail, axis, [(i, (i + 1) % count) for i in range(count)]),
                cells,
                lax.ppermute(head, axis, [((i + 1) % count, i) for i in range(count)]),
            ],
            axis=dim,
        )
    return cells


def body(velocity, counts, src_cell, weights, dst_cell, blade_tile, blade_cell, blade_coef):
    components = velocity.shape[0]
    cells_x = velocity.shape[1]
    cells_y = velocity.shape[2]
    levels = velocity.shape[3]
    total_cells = cells_x * cells_y * levels
    flat_vel = velocity.reshape(components, total_cells)
    count_y = lax.axis_size("gy")
    index_x = lax.axis_index("gx")
    index_y = lax.axis_index("gy")
    my_tile = index_x * count_y + index_y
    sampled = jnp.take(flat_vel, blade_cell, axis=1)
    owned = (blade_tile == my_tile)[None]
    sampled = jnp.where(owned, sampled, jnp.zeros_like(sampled))
    points = blade_cell.shape[1]
    points_x = lax.psum(sampled[0], ("gx", "gy"))
    rotor_mean = jnp.sum(points_x, axis=1) / points
    forces = -blade_coef[None] * rotor_mean[None, :, None] * sampled
    forcing = (
        jnp.zeros((components, total_cells), jnp.float32)
        .at[:, blade_cell.reshape(-1)]
        .add(forces.reshape(components, -1))
    )
    capacity = src_cell.shape[-1]
    active = lax.broadcasted_iota(jnp.int32, (9, capacity), 1) < counts[0, 0][:, None]
    masked_w = jnp.where(active, weights[0, 0], jnp.zeros_like(weights[0, 0]))
    picked = jnp.take(flat_vel, src_cell[0, 0].reshape(-1), axis=1).reshape(components, 9, capacity)
    blocks = jnp.concatenate([picked * masked_w[None], masked_w[None]], axis=0)
    grid_blocks = blocks.reshape(4, 3, 3, capacity)
    bordered = padded_2(grid_blocks, (("gx", 1), ("gy", 2)), 1)
    arrived = bordered[:, ::-2, ::-2].reshape(4, 9, capacity)
    targets = dst_cell[0, 0].reshape(-1)
    totals = jnp.zeros((4, total_cells), jnp.float32).at[:, targets].add(arrived.reshape(4, -1))
    corrected = (1.0 - totals[3]) * flat_vel - totals[:3]
    field_now = corrected.reshape(components, cells_x, cells_y, levels)
    padded = padded_2(field_now, (("gx", 1), ("gy", 2)), 1)
    padded = jnp.pad(padded, ((0, 0), (0, 0), (0, 0), (1, 1)))
    center = padded[:, 1:-1, 1:-1, 1:-1]
    east_side = padded[:, 2:, 1:-1, 1:-1]
    west_side = padded[:, :-2, 1:-1, 1:-1]
    north_side = padded[:, 1:-1, 2:, 1:-1]
    south_side = padded[:, 1:-1, :-2, 1:-1]
    upper_side = padded[:, 1:-1, 1:-1, 2:]
    lower_side = padded[:, 1:-1, 1:-1, :-2]
    laplace = (
        east_side + west_side + north_side + south_side + upper_side + lower_side - 6.0 * center
    )
    advection = (
        center[0:1] * (east_side - west_side) * 0.5
        + center[1:2] * (north_side - south_side) * 0.5
        + center[2:3] * (upper_side - lower_side) * 0.5
    )
    forcing_field = forcing.reshape(components, cells_x, cells_y, levels)
    updated = center + 0.2 * (0.15 * laplace - advection + forcing_field)
    return (updated, forcing_field)


def solution(mesh):
    placed = (
        P(None, "gx", "gy", None),
        P("gx", "gy", None),
        P("gx", "gy", None, None),
        P("gx", "gy", None, None),
        P("gx", "gy", None, None),
        P(),
        P(),
        P(),
    )
    return jax.shard_map(
        body,
        mesh=mesh,
        in_specs=placed,
        out_specs=(P(None, "gx", "gy", None), P(None, "gx", "gy", None)),
        check_vma=False,
    )
```

profile of v0, /device:TPU:1, one launch (start us, length us, event | category | flops | bytes accessed | tf_op | source)
XLA Modules:
  0.0 389.9 jit_solution(10842976870287354699)
XLA Ops:
  0.6 0.0 copy-start.2
  0.6 17.6 %copy.47 = f32[3,8,64,128]{0,3,2,1:T(8,128)} copy(f32[3,8,64,128]{3,2,1,0:T(8,128)} %param.8) | data formatting | bytes 1572864 | tf_op args[0]
  18.2 0.0 copy-start.7
  18.2 0.0 copy-start.3
  18.2 0.0 copy-start.4
  18.2 0.0 copy-start.1
  18.2 0.0 copy-done.2
  18.3 41.5 %gather_fusion = f32[9216,3]{1,0:T(8,128)} fusion(f32[3,65536]{0,1:T(8,128)} %bitcast.38, s32[9216]{0:T(1024)S(1)} %broadcast_clamp_fusion), kind=kCustom, calls=%fused_computation | custom fusion | bytes 258048 | tf_op jit(solution)/shard_map/jit(_take)/gather | solution.py:49
  59.8 0.0 copy-start.6
  59.8 3.1 copy.48
  62.9 0.1 reduce
  63.0 0.5 broadcast.151
  63.5 0.0 copy-done.7
  63.5 0.7 reduce.15
  64.2 0.1 lt.84
  64.2 0.0 copy-done.3
  64.2 0.1 reduce.2
  64.4 0.1 fusion.15
  64.5 0.1 compare_select_fusion.2
  64.6 0.1 select_multiply_fusion
  64.7 2.1 collective-permute-start
  66.8 3.1 collective-permute-start.1
  69.9 0.0 copy-done.4
  70.0 0.0 copy-done.1
  70.0 0.1 reshape.205
  70.1 16.8 %gather_fusion.1 = f32[3840,3]{1,0:T(8,128)S(1)} fusion(f32[3,65536]{0,1:T(8,128)} %bitcast.39, s32[4096]{0:T(1024)S(1)} %pad_clamp_fusion), kind=kCustom, calls=%fused_computation.1 | custom fusion | bytes 107520 | tf_op jit(solution)/shard_map/jit(_take)/gather | solution.py:34
  86.9 0.9 copy.56
  87.8 0.0 copy-done.6
  87.8 37.7 %psum.7 = f32[20,192]{1,0:T(8,128)S(1)} all-reduce(f32[20,192]{1,0:T(8,128)S(1)} %fusion.17), channel_id=1, replica_groups=mesh['gx'=8,'gy'=4] {'gx','gy'}, use_global_device_ids=true, to_apply=%region_1.2 | all-reduce | flops 3840 | bytes 30720 | tf_op jit(solution)/shard_map/psum | solution.py:38
  125.6 0.1 reduce_sum.9
  125.7 0.0 collective-permute-done
  125.7 0.0 collective-permute-done.1
  125.7 0.1 pad_maximum_fusion.12
  125.8 3.4 collective-permute-start.2
  129.2 0.0 collective-permute-start.3
  129.2 0.0 copy-done.5
  129.2 0.1 negate_multiply_fusion
  129.3 0.1 broadcast_in_dim.75
  129.3 0.1 broadcast_in_dim.77
  129.4 0.1 reshape.193
  129.5 0.1 mul.117
  129.6 1.8 collective-permute-done.2
  131.4 1.6 collective-permute-done.3
  133.0 0.1 pad_maximum_fusion.8
  133.2 3.0 copy.49
  136.2 62.9 %scatter_custom_fusion = f32[4,65536]{0,1:T(8,128)} fusion(s32[9216]{0:T(1024)S(1)} %bitcast.52, f32[9216,4]{1,0:T(8,128)} %copy.49, f32[]{:T(128)} %constant.18.clone.1), kind=kCustom, calls=%fused_computation.12 | custom fusion | flops 36864 | bytes 1049088 | tf_op jit(solution)/shard_map/scatter-add | solution.py:55
  199.1 20.3 %fusion = f32[65536]{0:T(1024)S(1)} fusion(f32[4,65536]{0,1:T(8,128)} %scatter_custom_fusion), kind=kLoop, calls=%fused_computation.9 | loop fusion | flops 65536 | bytes 524288 | tf_op jit(solution)/shard_map/sub | solution.py:56
  219.4 34.2 %slice_subtract_fusion = f32[3,65536]{0,1:T(8,128)} fusion(f32[4,65536]{0,1:T(8,128)} %scatter_custom_fusion, f32[65536]{0:T(1024)S(1)} %fusion, f32[3,8,64,128]{0,3,2,1:T(8,128)} %copy.47), kind=kLoop, calls=%fused_computation.7 | loop fusion | flops 393216 | bytes 2621440 | tf_op jit(solution)/shard_map/sub | solution.py:56
  253.6 19.5 %copy.59 = f32[3,8,64,128]{3,2,1,0:T(8,128)S(1)} copy(f32[3,8,64,128]{0,3,2,1:T(8,128)} %bitcast.37) | data formatting | bytes 1572864 | tf_op jit(solution)/shard_map/reshape | solution.py:57
  273.1 2.8 collective-permute-start.4
  276.0 0.0 collective-permute-start.5
  276.0 37.5 %scatter_custom_fusion.1 = f32[3,65536]{0,1:T(8,128)} fusion(s32[3840]{0:T(1024)S(1)} %fusion.18, f32[]{:T(128)} %constant.18.clone.1, f32[3840,3]{1,0:T(8,128)S(1)} %gather_fusion.1, f32[]{:T(128)} %constant.22.clone.1, f32[3840]{0:T(1024)S(1)} %mul.117, pred[3840]{0:T(1024)(128)(4,1)S(1)} %broadcast_in_dim.77, pred[3840]{0:T(1024)(128)(4,1)S(1)} %broadcast_in_dim.75), kind=kCustom, calls=%fused_computation.10 | custom fusion | flops 46080 | bytes 2778624 | tf_op jit(solution)/shard_map/scatter-add | solution.py:44
  313.5 19.5 %copy.58 = f32[3,8,64,128]{3,2,1,0:T(8,128)S(1)} copy(f32[3,8,64,128]{0,3,2,1:T(8,128)} %bitcast.40) | data formatting | bytes 1572864 | tf_op jit(solution)/shard_map/reshape | solution.py:75
  333.0 0.0 copy-start
  333.0 0.0 collective-permute-done.4
  333.0 0.0 collective-permute-done.5
  333.0 0.1 collective-permute-start.6
  333.1 1.7 collective-permute-start.7
  334.8 52.5 %slice_reduce_fusion.2 = (f32[65536]{0:T(1024)S(1)}, f32[65536]{0:T(1024)S(1)}, f32[65536]{0:T(1024)S(1)}) fusion(f32[3,65536]{0,1:T(8,128)} %slice_subtract_fusion), kind=kLoop, calls=%fused_computation.6 | loop fusion | bytes 1572864 | tf_op jit(solution)/shard_map/slice | solution.py:71
  387.3 0.0 collective-permute-done.6
  387.3 0.0 collective-permute-done.7
  387.3 0.8 select_maximum_fusion
  388.1 0.0 copy-done
  388.1 1.8 multiply_add_fusion
  (18 shorter events, 0.4 us)
Async XLA Ops:
  0.6 17.6 %copy-start.2 = (s32[1,1,9,1024]{3,1,2,0:T(1,128)S(1)}, s32[1,1,9,1024]{3,1,2,0:T(1,128)}, u32[]{:S(2)}) copy-start(s32[1,1,9,1024]{3,1,2,0:T(1,128)} %param.10) | copy-start | bytes 110596
  18.2 45.3 %copy-start.7 = (s32[1,1,9]{2,1,0:T(1,128)S(1)}, s32[1,1,9]{2,1,0:T(1,128)}, u32[]{:S(2)}) copy-start(s32[1,1,9]{2,1,0:T(1,128)} %param.9) | copy-start | bytes 112
  18.2 46.0 %copy-start.3 = (f32[1,1,9,1024]{3,1,2,0:T(1,128)S(1)}, f32[1,1,9,1024]{3,1,2,0:T(1,128)}, u32[]{:S(2)}) copy-start(f32[1,1,9,1024]{3,1,2,0:T(1,128)} %param.11) | copy-start | bytes 110596
  18.2 51.7 %copy-start.4 = (s32[1,1,9,1024]{3,1,2,0:T(1,128)S(1)}, s32[1,1,9,1024]{3,1,2,0:T(1,128)}, u32[]{:S(2)}) copy-start(s32[1,1,9,1024]{3,1,2,0:T(1,128)} %param.12) | copy-start | bytes 110596
  18.2 51.8 %copy-start.1 = (s32[20,192]{1,0:T(8,128)S(1)}, s32[20,192]{1,0:T(8,128)}, u32[]{:S(2)}) copy-start(s32[20,192]{1,0:T(8,128)} %param.14) | copy-start | bytes 46084
  59.8 28.0 %copy-start.6 = (s32[20,192]{1,0:T(8,128)S(1)}, s32[20,192]{1,0:T(8,128)}, u32[]{:S(2)}) copy-start(s32[20,192]{1,0:T(8,128)} %param.13) | copy-start | bytes 46084
  59.8 69.4 %copy-start.5 = (f32[20,192]{1,0:T(8,128)S(1)}, f32[20,192]{1,0:T(8,128)}, u32[]{:S(2)}) copy-start(f32[20,192]{1,0:T(8,128)} %param.15) | copy-start | bytes 46084
  64.7 61.0 %collective-permute-start = (f32[4,1,3,1024]{3,0,2,1:T(4,128)S(1)}, f32[4,1,3,1024]{3,0,2,1:T(4,128)S(1)}, u32[]{:S(2)}, u32[]{:S(2)}) collective-permute-start(f32[4,1,3,1024]{3,0,2,1:T(4,128)S(1)} %get-tuple-element.19), channel_id=1, source_target_pairs={{0,4},{4,8},{8,12},{12,16},{16,20},{20,24},{24,28},{28,0},{1,5},{5... | collective-permute-start | bytes 147464 | tf_op jit(solution)/shard_map/ppermute | solution.py:14
  66.8 58.9 %collective-permute-start.1 = (f32[4,1,3,1024]{3,0,2,1:T(4,128)S(1)}, f32[4,1,3,1024]{3,0,2,1:T(4,128)S(1)}, u32[]{:S(2)}, u32[]{:S(2)}) collective-permute-start(f32[4,1,3,1024]{3,0,2,1:T(4,128)S(1)} %get-tuple-element.20), channel_id=1, source_target_pairs={{4,0},{8,4},{12,8},{16,12},{20,16},{24,20},{28,24},{0,28},{5,1},{9... | collective-permute-start | bytes 147464 | tf_op jit(solution)/shard_map/ppermute | solution.py:16
  125.8 5.6 %collective-permute-start.2 = (f32[4,5,1,1024]{3,0,2,1:T(4,128)S(1)}, f32[4,5,1,1024]{3,0,2,1:T(4,128)S(1)}, u32[]{:S(2)}, u32[]{:S(2)}) collective-permute-start(f32[4,5,1,1024]{3,0,2,1:T(4,128)S(1)} %get-tuple-element.17), channel_id=1, source_target_pairs={{0,1},{1,2},{2,3},{3,0},{4,5},{5,6},{6,7},{7,4},{8,9},{9,10},{10,1... | collective-permute-start | bytes 245768 | tf_op jit(solution)/shard_map/ppermute | solution.py:14
  129.2 3.9 collective-permute-start.3
  273.1 59.8 %collective-permute-start.4 = (f32[3,1,64,128]{3,2,1,0:T(8,128)S(1)}, f32[3,1,64,128]{3,2,1,0:T(8,128)S(1)}, u32[]{:S(2)}, u32[]{:S(2)}) collective-permute-start(f32[3,1,64,128]{3,2,1,0:T(8,128)S(1)} %get-tuple-element.16), channel_id=1, source_target_pairs={{4,0},{8,4},{12,8},{16,12},{20,16},{24,20},{28,24},{0,28},{5,1},{9... | collective-permute-start | bytes 294920 | tf_op jit(solution)/shard_map/ppermute | solution.py:16
  276.0 57.0 %collective-permute-start.5 = (f32[3,1,64,128]{3,2,1,0:T(8,128)S(1)}, f32[3,1,64,128]{3,2,1,0:T(8,128)S(1)}, u32[]{:S(2)}, u32[]{:S(2)}) collective-permute-start(f32[3,1,64,128]{3,2,1,0:T(8,128)S(1)} %get-tuple-element.15), channel_id=1, source_target_pairs={{0,4},{4,8},{8,12},{12,16},{16,20},{20,24},{24,28},{28,0},{1,5},{5... | collective-permute-start | bytes 294920 | tf_op jit(solution)/shard_map/ppermute | solution.py:14
  333.0 55.2 %copy-start = (f32[3,8,64,128]{3,2,1,0:T(8,128)}, f32[3,8,64,128]{3,2,1,0:T(8,128)S(1)}, u32[]{:S(2)}) copy-start(f32[3,8,64,128]{3,2,1,0:T(8,128)S(1)} %copy.58) | copy-start | bytes 2359300
  333.0 54.3 %collective-permute-start.6 = (f32[3,10,1,128]{3,2,1,0:T(1,128)S(1)}, f32[3,10,1,128]{3,2,1,0:T(1,128)S(1)}, u32[]{:S(2)}, u32[]{:S(2)}) collective-permute-start(f32[3,10,1,128]{3,2,1,0:T(1,128)S(1)} %get-tuple-element.14), channel_id=1, source_target_pairs={{1,0},{2,1},{3,2},{0,3},{5,4},{6,5},{7,6},{4,7},{9,8},{10,9},{11,1... | collective-permute-start | bytes 46088 | tf_op jit(solution)/shard_map/ppermute | solution.py:16
  333.1 54.2 %collective-permute-start.7 = (f32[3,10,1,128]{3,2,1,0:T(1,128)S(1)}, f32[3,10,1,128]{3,2,1,0:T(1,128)S(1)}, u32[]{:S(2)}, u32[]{:S(2)}) collective-permute-start(f32[3,10,1,128]{3,2,1,0:T(1,128)S(1)} %get-tuple-element.13), channel_id=1, source_target_pairs={{0,1},{1,2},{2,3},{3,0},{4,5},{5,6},{6,7},{7,4},{8,9},{9,10},{10,1... | collective-permute-start | bytes 46088 | tf_op jit(solution)/shard_map/ppermute | solution.py:14
where the time goes:
time: 391 us; the launch traced here: 390 us
  local copies, waits for them, and re-layouts  175 us (45%)
  other arithmetic  159 us (41%)
  blocking collectives  37.7 us (10%)
  starting transfers between devices  13.2 us (3%)
    scatter-add x1, other arithmetic, body(): jnp.zeros((4, total_cells), jnp.float32).at[:, targets]  62.9 us
    sub x2, other arithmetic, body(): corrected = (1.0 - totals[3]) * flat_vel - totals[:3]  54.5 us
    slice x1, local copies, waits for them, and re-layouts, body(): center[0:1] * (east_side - west_side) * 0.5  52.5 us
    gather x2, local copies, waits for them, and re-layouts, body(): jnp.take(flat_vel, src_cell[0, 0].reshape(-1), axis=1)  44.6 us
    psum x1, blocking collectives, body(): points_x = lax.psum(sampled[0], ('gx', 'gy'))  37.7 us
    scatter-add x1, other arithmetic, body(): forcing = jnp.zeros((components, total_cells), jnp.float32).at[:, blade_c...  37.5 us
    reshape x1, local copies, waits for them, and re-layouts, body(): field_now = corrected.reshape(components, cells_x, cells_y, levels)  19.5 us
    reshape x1, local copies, waits for them, and re-layouts, body(): forcing_field = forcing.reshape(components, cells_x, cells_y, levels)  19.5 us
  transfers between devices with their start and end apart: 8, of which 2 were waited for; matrix products, arithmetic and copies ran while one was open for 33% of the time, Pallas kernels for 0%

commit v1 on v0

--- a/solution.py
+++ b/solution.py
@@ -35,7 +35,9 @@
     owned = (blade_tile == my_tile)[None]
     sampled = jnp.where(owned, sampled, jnp.zeros_like(sampled))
     points = blade_cell.shape[1]
-    points_x = lax.psum(sampled[0], ("gx", "gy"))
+    matrix = sampled[0]
+    before = lax.psum(matrix, "gy")
+    points_x = lax.psum(before, "gx")
     rotor_mean = jnp.sum(points_x, axis=1) / points
     forces = -blade_coef[None] * rotor_mean[None, :, None] * sampled
     forcing = (

time: 391 us -> 396 us (1.013)
  starting transfers between devices: 13.2 us -> 17.5 us
    ppermute x4, starting transfers between devices: 7.2 us -> 14.3 us  [padded_2(): lax.ppermute(tail, axis, [(i, (i + 1) % count) for i in range(count)])]
    psum x1 -> x2, blocking collectives: 37.7 us -> 38.3 us  [the longest x1 27.5 us: body(): points_x = lax.psum(before, 'gx')]
  transfers between devices with their start and end apart: 8 -> 8, of which waited for: 2 -> 2; matrix products, arithmetic and copies ran while one was open for 33% -> 32% of each run, Pallas kernels for 0% -> 0%
where the time goes in v1:
time: 396 us; the launch traced here: 395 us
  local copies, waits for them, and re-layouts  175 us (44%)
  other arithmetic  159 us (40%)
  blocking collectives  38.3 us (10%)
  starting transfers between devices  17.5 us (4%)
    scatter-add x1, other arithmetic, body(): jnp.zeros((4, total_cells), jnp.float32).at[:, targets]  62.9 us
    sub x2, other arithmetic, body(): corrected = (1.0 - totals[3]) * flat_vel - totals[:3]  54.5 us
    slice x1, local copies, waits for them, and re-layouts, body(): center[0:1] * (east_side - west_side) * 0.5  52.5 us
    gather x2, local copies, waits for them, and re-layouts, body(): jnp.take(flat_vel, src_cell[0, 0].reshape(-1), axis=1)  44.6 us
    scatter-add x1, other arithmetic, body(): forcing = jnp.zeros((components, total_cells), jnp.float32).at[:, blade_c...  37.5 us
    psum x1, blocking collectives, body(): points_x = lax.psum(before, 'gx')  27.5 us
    reshape x1, local copies, waits for them, and re-layouts, body(): field_now = corrected.reshape(components, cells_x, cells_y, levels)  19.5 us
    reshape x1, local copies, waits for them, and re-layouts, body(): forcing_field = forcing.reshape(components, cells_x, cells_y, levels)  19.5 us
  transfers between devices with their start and end apart: 8, of which 2 were waited for; matrix products, arithmetic and copies ran while one was open for 32% of the time, Pallas kernels for 0%

profile of v1, /device:TPU:1, one launch (start us, length us, event | category | flops | bytes accessed | tf_op | source)
XLA Modules:
  0.0 394.8 jit_solution(8664108280674274974)
XLA Ops:
  0.6 0.0 copy-start.2
  0.6 17.6 %copy.47 = f32[3,8,64,128]{0,3,2,1:T(8,128)} copy(f32[3,8,64,128]{3,2,1,0:T(8,128)} %param.8) | data formatting | bytes 1572864 | tf_op args[0]
  18.2 0.0 copy-start.7
  18.2 0.0 copy-start.3
  18.2 0.0 copy-start.4
  18.2 0.0 copy-start.1
  18.2 0.0 copy-done.2
  18.3 41.5 %gather_fusion = f32[9216,3]{1,0:T(8,128)} fusion(f32[3,65536]{0,1:T(8,128)} %bitcast.38, s32[9216]{0:T(1024)S(1)} %broadcast_clamp_fusion), kind=kCustom, calls=%fused_computation | custom fusion | bytes 258048 | tf_op jit(solution)/shard_map/jit(_take)/gather | solution.py:51
  59.8 3.1 copy.48
  62.9 0.1 reduce
  63.0 0.5 broadcast.151
  63.5 0.0 copy-done.7
  63.5 0.7 reduce.15
  64.2 0.1 lt.84
  64.2 0.0 copy-done.3
  64.2 0.1 reduce.2
  64.4 0.1 fusion.15
  64.5 0.1 compare_select_fusion.2
  64.6 0.1 select_multiply_fusion
  64.7 2.1 collective-permute-start
  66.8 3.1 collective-permute-start.1
  69.9 0.0 copy-done.4
  70.0 0.0 copy-done.1
  70.0 0.1 reshape.205
  70.1 16.8 %gather_fusion.1 = f32[3840,3]{1,0:T(8,128)S(1)} fusion(f32[3,65536]{0,1:T(8,128)} %bitcast.39, s32[4096]{0:T(1024)S(1)} %pad_clamp_fusion), kind=kCustom, calls=%fused_computation.1 | custom fusion | bytes 107520 | tf_op jit(solution)/shard_map/jit(_take)/gather | solution.py:34
  86.9 0.9 copy.56
  87.8 0.0 copy-done.6
  87.8 10.8 %psum.14 = f32[20,192]{1,0:T(8,128)S(1)} all-reduce(f32[20,192]{1,0:T(8,128)S(1)} %fusion.17), channel_id=1, replica_groups=mesh['gx'=8,'gy'=4] {'gy'}, use_global_device_ids=true, to_apply=%region_1.2 | all-reduce | flops 3840 | bytes 30720 | tf_op jit(solution)/shard_map/psum | solution.py:39
  98.6 27.5 %psum.15 = f32[20,192]{1,0:T(8,128)S(1)} all-reduce(f32[20,192]{1,0:T(8,128)S(1)} %psum.14), channel_id=1, replica_groups=mesh['gx'=8,'gy'=4] {'gx'}, use_global_device_ids=true, to_apply=%region_2.3 | all-reduce | flops 3840 | bytes 30720 | tf_op jit(solution)/shard_map/psum | solution.py:40
  126.1 0.1 reduce_sum.9
  126.3 0.0 collective-permute-done
  126.3 0.0 collective-permute-done.1
  126.3 0.1 pad_maximum_fusion.12
  126.4 9.0 %collective-permute-start.2 = (f32[4,5,1,1024]{3,0,2,1:T(4,128)S(1)}, f32[4,5,1,1024]{3,0,2,1:T(4,128)S(1)}, u32[]{:S(2)}, u32[]{:S(2)}) collective-permute-start(f32[4,5,1,1024]{3,0,2,1:T(4,128)S(1)} %get-tuple-element.17), channel_id=1, source_target_pairs={{0,1},{1,2},{2,3},{3,0},{4,5},{5,6},{6,7},{7,4},{8,9},{9,10},{10,1... | collective-permute-start | bytes 245768 | tf_op jit(solution)/shard_map/ppermute | solution.py:14
  135.3 0.0 collective-permute-start.3
  135.4 0.0 copy-done.5
  135.4 0.1 negate_multiply_fusion
  135.4 0.1 broadcast_in_dim.75
  135.5 0.1 broadcast_in_dim.77
  135.6 0.1 reshape.193
  135.7 0.1 mul.117
  135.8 1.1 collective-permute-done.2
  136.8 2.4 collective-permute-done.3
  139.2 0.1 pad_maximum_fusion.8
  139.4 3.0 copy.49
  142.4 62.9 %scatter_custom_fusion = f32[4,65536]{0,1:T(8,128)} fusion(s32[9216]{0:T(1024)S(1)} %bitcast.52, f32[9216,4]{1,0:T(8,128)} %copy.49, f32[]{:T(128)} %constant.18.clone.1), kind=kCustom, calls=%fused_computation.12 | custom fusion | flops 36864 | bytes 1049088 | tf_op jit(solution)/shard_map/scatter-add | solution.py:57
  205.3 20.3 %fusion = f32[65536]{0:T(1024)S(1)} fusion(f32[4,65536]{0,1:T(8,128)} %scatter_custom_fusion), kind=kLoop, calls=%fused_computation.9 | loop fusion | flops 65536 | bytes 524288 | tf_op jit(solution)/shard_map/sub | solution.py:58
  225.6 34.2 %slice_subtract_fusion = f32[3,65536]{0,1:T(8,128)} fusion(f32[4,65536]{0,1:T(8,128)} %scatter_custom_fusion, f32[65536]{0:T(1024)S(1)} %fusion, f32[3,8,64,128]{0,3,2,1:T(8,128)} %copy.47), kind=kLoop, calls=%fused_computation.7 | loop fusion | flops 393216 | bytes 2621440 | tf_op jit(solution)/shard_map/sub | solution.py:58
  259.8 19.5 %copy.59 = f32[3,8,64,128]{3,2,1,0:T(8,128)S(1)} copy(f32[3,8,64,128]{0,3,2,1:T(8,128)} %bitcast.37) | data formatting | bytes 1572864 | tf_op jit(solution)/shard_map/reshape | solution.py:59
  279.3 0.1 collective-permute-start.4
  279.4 1.5 collective-permute-start.5
  280.9 37.5 %scatter_custom_fusion.1 = f32[3,65536]{0,1:T(8,128)} fusion(s32[3840]{0:T(1024)S(1)} %fusion.18, f32[]{:T(128)} %constant.18.clone.1, f32[3840,3]{1,0:T(8,128)S(1)} %gather_fusion.1, f32[]{:T(128)} %constant.22.clone.1, f32[3840]{0:T(1024)S(1)} %mul.117, pred[3840]{0:T(1024)(128)(4,1)S(1)} %broadcast_in_dim.77, pred[3840]{0:T(1024)(128)(4,1)S(1)} %broadcast_in_dim.75), kind=kCustom, calls=%fused_computation.10 | custom fusion | flops 46080 | bytes 2778624 | tf_op jit(solution)/shard_map/scatter-add | solution.py:46
  318.3 19.5 %copy.58 = f32[3,8,64,128]{3,2,1,0:T(8,128)S(1)} copy(f32[3,8,64,128]{0,3,2,1:T(8,128)} %bitcast.40) | data formatting | bytes 1572864 | tf_op jit(solution)/shard_map/reshape | solution.py:77
  337.8 0.0 copy-start
  337.8 0.0 collective-permute-done.4
  337.8 0.0 collective-permute-done.5
  337.9 0.1 collective-permute-start.6
  337.9 1.7 collective-permute-start.7
  339.7 52.5 %slice_reduce_fusion.2 = (f32[65536]{0:T(1024)S(1)}, f32[65536]{0:T(1024)S(1)}, f32[65536]{0:T(1024)S(1)}) fusion(f32[3,65536]{0,1:T(8,128)} %slice_subtract_fusion), kind=kLoop, calls=%fused_computation.6 | loop fusion | bytes 1572864 | tf_op jit(solution)/shard_map/slice | solution.py:73
  392.2 0.0 collective-permute-done.6
  392.2 0.0 collective-permute-done.7
  392.2 0.8 select_maximum_fusion
  393.0 0.0 copy-done
  393.0 1.8 multiply_add_fusion
  (19 shorter events, 0.4 us)
Async XLA Ops:
  0.6 17.6 %copy-start.2 = (s32[1,1,9,1024]{3,1,2,0:T(1,128)S(1)}, s32[1,1,9,1024]{3,1,2,0:T(1,128)}, u32[]{:S(2)}) copy-start(s32[1,1,9,1024]{3,1,2,0:T(1,128)} %param.10) | copy-start | bytes 110596
  18.2 45.3 %copy-start.7 = (s32[1,1,9]{2,1,0:T(1,128)S(1)}, s32[1,1,9]{2,1,0:T(1,128)}, u32[]{:S(2)}) copy-start(s32[1,1,9]{2,1,0:T(1,128)} %param.9) | copy-start | bytes 112
  18.2 46.0 %copy-start.3 = (f32[1,1,9,1024]{3,1,2,0:T(1,128)S(1)}, f32[1,1,9,1024]{3,1,2,0:T(1,128)}, u32[]{:S(2)}) copy-start(f32[1,1,9,1024]{3,1,2,0:T(1,128)} %param.11) | copy-start | bytes 110596
  18.2 51.7 %copy-start.4 = (s32[1,1,9,1024]{3,1,2,0:T(1,128)S(1)}, s32[1,1,9,1024]{3,1,2,0:T(1,128)}, u32[]{:S(2)}) copy-start(s32[1,1,9,1024]{3,1,2,0:T(1,128)} %param.12) | copy-start | bytes 110596
  18.2 51.8 %copy-start.1 = (s32[20,192]{1,0:T(8,128)S(1)}, s32[20,192]{1,0:T(8,128)}, u32[]{:S(2)}) copy-start(s32[20,192]{1,0:T(8,128)} %param.14) | copy-start | bytes 46084
  59.8 28.0 %copy-start.6 = (s32[20,192]{1,0:T(8,128)S(1)}, s32[20,192]{1,0:T(8,128)}, u32[]{:S(2)}) copy-start(s32[20,192]{1,0:T(8,128)} %param.13) | copy-start | bytes 46084
  59.8 75.6 %copy-start.5 = (f32[20,192]{1,0:T(8,128)S(1)}, f32[20,192]{1,0:T(8,128)}, u32[]{:S(2)}) copy-start(f32[20,192]{1,0:T(8,128)} %param.15) | copy-start | bytes 46084
  64.7 61.5 %collective-permute-start = (f32[4,1,3,1024]{3,0,2,1:T(4,128)S(1)}, f32[4,1,3,1024]{3,0,2,1:T(4,128)S(1)}, u32[]{:S(2)}, u32[]{:S(2)}) collective-permute-start(f32[4,1,3,1024]{3,0,2,1:T(4,128)S(1)} %get-tuple-element.19), channel_id=1, source_target_pairs={{0,4},{4,8},{8,12},{12,16},{16,20},{20,24},{24,28},{28,0},{1,5},{5... | collective-permute-start | bytes 147464 | tf_op jit(solution)/shard_map/ppermute | solution.py:14
  66.8 59.4 %collective-permute-start.1 = (f32[4,1,3,1024]{3,0,2,1:T(4,128)S(1)}, f32[4,1,3,1024]{3,0,2,1:T(4,128)S(1)}, u32[]{:S(2)}, u32[]{:S(2)}) collective-permute-start(f32[4,1,3,1024]{3,0,2,1:T(4,128)S(1)} %get-tuple-element.20), channel_id=1, source_target_pairs={{4,0},{8,4},{12,8},{16,12},{20,16},{24,20},{28,24},{0,28},{5,1},{9... | collective-permute-start | bytes 147464 | tf_op jit(solution)/shard_map/ppermute | solution.py:16
  126.4 10.5 %collective-permute-start.2 = (f32[4,5,1,1024]{3,0,2,1:T(4,128)S(1)}, f32[4,5,1,1024]{3,0,2,1:T(4,128)S(1)}, u32[]{:S(2)}, u32[]{:S(2)}) collective-permute-start(f32[4,5,1,1024]{3,0,2,1:T(4,128)S(1)} %get-tuple-element.17), channel_id=1, source_target_pairs={{0,1},{1,2},{2,3},{3,0},{4,5},{5,6},{6,7},{7,4},{8,9},{9,10},{10,1... | collective-permute-start | bytes 245768 | tf_op jit(solution)/shard_map/ppermute | solution.py:14
  135.3 3.9 collective-permute-start.3
  279.3 58.5 %collective-permute-start.4 = (f32[3,1,64,128]{3,2,1,0:T(8,128)S(1)}, f32[3,1,64,128]{3,2,1,0:T(8,128)S(1)}, u32[]{:S(2)}, u32[]{:S(2)}) collective-permute-start(f32[3,1,64,128]{3,2,1,0:T(8,128)S(1)} %get-tuple-element.16), channel_id=1, source_target_pairs={{4,0},{8,4},{12,8},{16,12},{20,16},{24,20},{28,24},{0,28},{5,1},{9... | collective-permute-start | bytes 294920 | tf_op jit(solution)/shard_map/ppermute | solution.py:16
  279.4 58.5 %collective-permute-start.5 = (f32[3,1,64,128]{3,2,1,0:T(8,128)S(1)}, f32[3,1,64,128]{3,2,1,0:T(8,128)S(1)}, u32[]{:S(2)}, u32[]{:S(2)}) collective-permute-start(f32[3,1,64,128]{3,2,1,0:T(8,128)S(1)} %get-tuple-element.15), channel_id=1, source_target_pairs={{0,4},{4,8},{8,12},{12,16},{16,20},{20,24},{24,28},{28,0},{1,5},{5... | collective-permute-start | bytes 294920 | tf_op jit(solution)/shard_map/ppermute | solution.py:14
  337.8 55.2 %copy-start = (f32[3,8,64,128]{3,2,1,0:T(8,128)}, f32[3,8,64,128]{3,2,1,0:T(8,128)S(1)}, u32[]{:S(2)}) copy-start(f32[3,8,64,128]{3,2,1,0:T(8,128)S(1)} %copy.58) | copy-start | bytes 2359300
  337.9 54.3 %collective-permute-start.6 = (f32[3,10,1,128]{3,2,1,0:T(1,128)S(1)}, f32[3,10,1,128]{3,2,1,0:T(1,128)S(1)}, u32[]{:S(2)}, u32[]{:S(2)}) collective-permute-start(f32[3,10,1,128]{3,2,1,0:T(1,128)S(1)} %get-tuple-element.14), channel_id=1, source_target_pairs={{1,0},{2,1},{3,2},{0,3},{5,4},{6,5},{7,6},{4,7},{9,8},{10,9},{11,1... | collective-permute-start | bytes 46088 | tf_op jit(solution)/shard_map/ppermute | solution.py:16
  337.9 54.2 %collective-permute-start.7 = (f32[3,10,1,128]{3,2,1,0:T(1,128)S(1)}, f32[3,10,1,128]{3,2,1,0:T(1,128)S(1)}, u32[]{:S(2)}, u32[]{:S(2)}) collective-permute-start(f32[3,10,1,128]{3,2,1,0:T(1,128)S(1)} %get-tuple-element.13), channel_id=1, source_target_pairs={{0,1},{1,2},{2,3},{3,0},{4,5},{5,6},{6,7},{7,4},{8,9},{9,10},{10,1... | collective-permute-start | bytes 46088 | tf_op jit(solution)/shard_map/ppermute | solution.py:14
